TPU v7x, 512 devices: a whole 4x8x8 slice. The times are simulated.
512 devices in a mesh: row: 16 (over z, core), col: 32 (over x, y).
Axes of the slice: x: 4, y: 8, z: 8, core: 2. Of those that a mesh axis runs over, the one named last changes fastest.
Arguments:
- panels: float32 [8192, 16384], P('row', 'col'), as said below
Outputs:
- r_rows: float32 [256, 16384], P(None, 'col')
Inputs may be any that keep to these rules, and one draw needn't show every extreme that they name: `panels`: the first 256 columns of W have full column rank.
All inputs are finite; a program needn't handle non-finite values.
Results may differ from a plain program's by a relative error of at most 0.0003.
Values sent between devices are 32-bit elements; how exact they have to be, the bound alone decides.
A program may use at most 64 MiB of HBM per device.

v0:
```python
import jax
import jax.numpy as jnp
from jax import lax
from jax.sharding import PartitionSpec as P

PANEL = 128


def swapped(shard, axis, distance):
    return lax.ppermute(shard, axis, [(i, i ^ 1 << distance) for i in range(lax.axis_size(axis))])


def spread_2(block, axis, source):
    block = jnp.where(lax.axis_index(axis) == source, block, jnp.zeros_like(block))
    return lax.psum(block, axis)


def matmul(left, right):
    return jnp.dot(left, right, precision=lax.Precision.HIGHEST, preferred_element_type=jnp.float32)


def contract_rows(left, right):
    return lax.dot_general(
        left,
        right,
        (((0,), (0,)), ((), ())),
        precision=lax.Precision.HIGHEST,
        preferred_element_type=jnp.float32,
    )


def outer_rows(left, right):
    return lax.dot_general(
        left,
        right,
        (((1,), (1,)), ((), ())),
        precision=lax.Precision.HIGHEST,
        preferred_element_type=jnp.float32,
    )


def factor(columns):
    first_low = jnp.linalg.cholesky(contract_rows(columns, columns))
    basis_one = jax.scipy.linalg.solve_triangular(first_low, columns.T, lower=True)
    second_low = jnp.linalg.cholesky(outer_rows(basis_one, basis_one))
    basis_t = jax.scipy.linalg.solve_triangular(second_low, basis_one, lower=True)
    triangle = matmul(first_low, second_low).T
    return (basis_t, triangle)


def lower_side(level_bit):
    return lax.axis_index("row") >> level_bit & 1 == 0


def stack_pair(mine, other, is_lower):
    return jnp.concatenate(
        [jnp.where(is_lower, mine, other), jnp.where(is_lower, other, mine)], axis=0
    )


def own_half(level_basis, is_lower):
    start = jnp.where(is_lower, 0, PANEL).astype(jnp.int32)
    return lax.dynamic_slice_in_dim(level_basis, start, PANEL, 1)


def spread_back(halves, top_rows, basis_t, working):
    spread = top_rows
    for my_half in reversed(halves):
        spread = contract_rows(my_half, spread)
    return working - contract_rows(basis_t, spread)


def owner_step(working, panels, panel_index):
    depth_count = lax.axis_size("row").bit_length() - 1
    is_owner = lax.axis_index("col") == panel_index
    columns = jnp.where(is_owner, working[:, :PANEL], panels[:, :PANEL])
    basis_t, triangle = factor(columns)
    level_list = []
    for level_bit in range(depth_count):
        other_tri = swapped(triangle, "row", level_bit)
        level_basis, triangle = factor(stack_pair(triangle, other_tri, lower_side(level_bit)))
        level_list.append(level_basis)
    basis_t, level_stack = (
        spread_2(basis_t, "col", panel_index),
        spread_2(jnp.stack(level_list), "col", panel_index),
    )
    top_rows = matmul(basis_t, working)
    halves = []
    for level_bit in range(depth_count):
        other_top = swapped(top_rows, "row", level_bit)
        is_lower = lower_side(level_bit)
        top_rows = matmul(level_stack[level_bit], stack_pair(top_rows, other_top, is_lower))
        halves.append(own_half(level_stack[level_bit], is_lower))
    return (top_rows, spread_back(halves, top_rows, basis_t, working))


def local(panels):
    working = panels
    pieces = []
    for panel_index in range(2):
        top_rows, working = owner_step(working, panels, panel_index)
        pieces.append(top_rows)
    top_block = jnp.concatenate(pieces, axis=0)
    local_width = panels.shape[1]
    col_iota = jnp.arange(local_width, dtype=jnp.int32)
    global_col = (
        col_iota // PANEL * lax.axis_size("col") + lax.axis_index("col")
    ) * PANEL + col_iota % PANEL
    row_iota = jnp.arange(2 * PANEL, dtype=jnp.int32)
    keep_mask = global_col[None, :] >= row_iota[:, None]
    return jnp.where(keep_mask, top_block, jnp.zeros_like(top_block))


def solution(mesh):
    return jax.shard_map(
        local,
        mesh=mesh,
        in_specs=(P("row", "col"),),
        out_specs=P(None, "col"),
        check_vma=False,
    )
```

profile of v0, /device:TPU:1, one launch (start us, length us, event | category | flops | bytes accessed | tf_op | source)
XLA Modules:
  0.0 1003.0 jit_solution(15096186413171939091)
XLA Ops:
  8.3 11.7 %cholesky.314 = f32[128,128]{1,0:T(8,128)S(1)} custom-call(f32[128,128]{1,0:T(8,128)S(1)} %fusion.119), custom_call_target="Cholesky" | custom-call | tf_op jit(solution)/shard_map/jit(cholesky)/cholesky | solution.py:43
  33.0 11.7 %cholesky.325 = f32[128,128]{1,0:T(8,128)S(1)} custom-call(f32[128,128]{1,0:T(8,128)S(1)} %fusion.117), custom_call_target="Cholesky" | custom-call | tf_op jit(solution)/shard_map/jit(cholesky)/cholesky | solution.py:45
  68.3 11.7 %cholesky.336 = f32[128,128]{1,0:T(8,128)S(1)} custom-call(f32[128,128]{1,0:T(8,128)S(1)} %fusion.116), custom_call_target="Cholesky" | custom-call | tf_op jit(solution)/shard_map/jit(cholesky)/cholesky | solution.py:43
  91.9 22.8 %cholesky.347 = f32[128,128]{1,0:T(8,128)S(1)} custom-call(f32[128,128]{1,0:T(8,128)S(1)} %fusion.114), custom_call_target="Cholesky" | custom-call | tf_op jit(solution)/shard_map/jit(cholesky)/cholesky | solution.py:45
  133.6 11.7 %cholesky.358 = f32[128,128]{1,0:T(8,128)S(1)} custom-call(f32[128,128]{1,0:T(8,128)S(1)} %fusion.112), custom_call_target="Cholesky" | custom-call | tf_op jit(solution)/shard_map/jit(cholesky)/cholesky | solution.py:43
  157.2 11.7 %cholesky.369 = f32[128,128]{1,0:T(8,128)S(1)} custom-call(f32[128,128]{1,0:T(8,128)S(1)} %fusion.110), custom_call_target="Cholesky" | custom-call | tf_op jit(solution)/shard_map/jit(cholesky)/cholesky | solution.py:45
  172.0 10.2 %custom-call.30 = f32[1,128,128]{1,2,0:T(8,128)S(1)} custom-call(f32[1,128,128]{2,1,0:T(8,128)S(1)} %select_bitcast_fusion.11), custom_call_target="InvertDiagBlocksLowerTriangular" | custom-call | tf_op jit(solution)/shard_map/jit(_solve_triangular)/triangular_solve | solution.py:46
  190.7 11.7 %cholesky.380 = f32[128,128]{1,0:T(8,128)S(1)} custom-call(f32[128,128]{1,0:T(8,128)S(1)} %fusion.108), custom_call_target="Cholesky" | custom-call | tf_op jit(solution)/shard_map/jit(cholesky)/cholesky | solution.py:43
  214.3 11.7 %cholesky.391 = f32[128,128]{1,0:T(8,128)S(1)} custom-call(f32[128,128]{1,0:T(8,128)S(1)} %fusion.106), custom_call_target="Cholesky" | custom-call | tf_op jit(solution)/shard_map/jit(cholesky)/cholesky | solution.py:45
  229.1 10.0 custom-call.32
  248.5 11.7 %cholesky.402 = f32[128,128]{1,0:T(8,128)S(1)} custom-call(f32[128,128]{1,0:T(8,128)S(1)} %fusion.104), custom_call_target="Cholesky" | custom-call | tf_op jit(solution)/shard_map/jit(cholesky)/cholesky | solution.py:43
  272.1 11.7 %cholesky.413 = f32[128,128]{1,0:T(8,128)S(1)} custom-call(f32[128,128]{1,0:T(8,128)S(1)} %fusion.102), custom_call_target="Cholesky" | custom-call | tf_op jit(solution)/shard_map/jit(cholesky)/cholesky | solution.py:45
  285.1 10.2 %custom-call.34 = f32[1,128,128]{1,2,0:T(8,128)S(1)} custom-call(f32[1,128,128]{2,1,0:T(8,128)S(1)} %fusion.69), custom_call_target="InvertDiagBlocksLowerTriangular" | custom-call | tf_op jit(solution)/shard_map/jit(_solve_triangular)/triangular_solve | solution.py:46
  296.6 156.7 %all-reduce.7.cloned.1.call-done = (f32[128,512]{1,0:T(8,128)}, f32[4,128,256]{2,1,0:T(8,128)}) async-done(((f32[128,512]{1,0:T(8,128)}, f32[4,128,256]{2,1,0:T(8,128)}), (f32[128,512]{1,0:T(8,128)}, f32[4,128,256]{2,1,0:T(8,128)})) %all-reduce.7.cloned.1.call-update) | async-done | bytes 786448 | tf_op jit(solution)/shard_map/psum | solution.py:15
  478.3 11.3 %collective-permute-done.6 = f32[128,512]{1,0:T(8,128)S(1)} collective-permute-done((f32[128,512]{1,0:T(8,128)S(1)}, f32[128,512]{1,0:T(8,128)S(1)}, u32[]{:S(2)}, u32[]{:S(2)}) %collective-permute-start.6) | collective-permute-done | bytes 262176 | tf_op jit(solution)/shard_map/ppermute | solution.py:10
  498.6 11.5 %collective-permute-done.7 = f32[128,512]{1,0:T(8,128)S(1)} collective-permute-done((f32[128,512]{1,0:T(8,128)S(1)}, f32[128,512]{1,0:T(8,128)S(1)}, u32[]{:S(2)}, u32[]{:S(2)}) %collective-permute-start.7) | collective-permute-done | bytes 262176 | tf_op jit(solution)/shard_map/ppermute | solution.py:10
  514.7 11.7 %cholesky.424 = f32[128,128]{1,0:T(8,128)S(1)} custom-call(f32[128,128]{1,0:T(8,128)S(1)} %fusion.91), custom_call_target="Cholesky" | custom-call | tf_op jit(solution)/shard_map/jit(cholesky)/cholesky | solution.py:43
  538.5 11.9 %cholesky.435 = f32[128,128]{1,0:T(8,128)S(1)} custom-call(f32[128,128]{1,0:T(8,128)S(1)} %fusion.89), custom_call_target="Cholesky" | custom-call | tf_op jit(solution)/shard_map/jit(cholesky)/cholesky | solution.py:45
  568.2 11.7 %cholesky.446 = f32[128,128]{1,0:T(8,128)S(1)} custom-call(f32[128,128]{1,0:T(8,128)S(1)} %fusion.88), custom_call_target="Cholesky" | custom-call | tf_op jit(solution)/shard_map/jit(cholesky)/cholesky | solution.py:43
  591.8 12.1 %cholesky.457 = f32[128,128]{1,0:T(8,128)S(1)} custom-call(f32[128,128]{1,0:T(8,128)S(1)} %fusion.86), custom_call_target="Cholesky" | custom-call | tf_op jit(solution)/shard_map/jit(cholesky)/cholesky | solution.py:45
  622.8 11.7 %cholesky.468 = f32[128,128]{1,0:T(8,128)S(1)} custom-call(f32[128,128]{1,0:T(8,128)S(1)} %fusion.84), custom_call_target="Cholesky" | custom-call | tf_op jit(solution)/shard_map/jit(cholesky)/cholesky | solution.py:43
  646.4 11.7 %cholesky.479 = f32[128,128]{1,0:T(8,128)S(1)} custom-call(f32[128,128]{1,0:T(8,128)S(1)} %fusion.82), custom_call_target="Cholesky" | custom-call | tf_op jit(solution)/shard_map/jit(cholesky)/cholesky | solution.py:45
  661.2 10.0 custom-call.40
  679.5 11.7 %cholesky.490 = f32[128,128]{1,0:T(8,128)S(1)} custom-call(f32[128,128]{1,0:T(8,128)S(1)} %fusion.80), custom_call_target="Cholesky" | custom-call | tf_op jit(solution)/shard_map/jit(cholesky)/cholesky | solution.py:43
  703.1 11.7 %cholesky.501 = f32[128,128]{1,0:T(8,128)S(1)} custom-call(f32[128,128]{1,0:T(8,128)S(1)} %fusion.78), custom_call_target="Cholesky" | custom-call | tf_op jit(solution)/shard_map/jit(cholesky)/cholesky | solution.py:45
  717.9 10.0 custom-call.42
  738.4 11.7 %cholesky.512 = f32[128,128]{1,0:T(8,128)S(1)} custom-call(f32[128,128]{1,0:T(8,128)S(1)} %fusion.76), custom_call_target="Cholesky" | custom-call | tf_op jit(solution)/shard_map/jit(cholesky)/cholesky | solution.py:43
  761.9 11.7 %cholesky.523 = f32[128,128]{1,0:T(8,128)S(1)} custom-call(f32[128,128]{1,0:T(8,128)S(1)} %fusion.74), custom_call_target="Cholesky" | custom-call | tf_op jit(solution)/shard_map/jit(cholesky)/cholesky | solution.py:45
  775.0 10.0 custom-call.44
  786.2 151.2 %all-reduce.5.cloned.1.call-done = (f32[128,512]{1,0:T(8,128)}, f32[4,128,256]{2,1,0:T(8,128)}) async-done(((f32[128,512]{1,0:T(8,128)}, f32[4,128,256]{2,1,0:T(8,128)}), (f32[128,512]{1,0:T(8,128)}, f32[4,128,256]{2,1,0:T(8,128)})) %all-reduce.5.cloned.1.call-update) | async-done | bytes 786448 | tf_op jit(solution)/shard_map/psum | solution.py:15
  962.5 11.3 %collective-permute-done.14 = f32[128,512]{1,0:T(8,128)S(1)} collective-permute-done((f32[128,512]{1,0:T(8,128)S(1)}, f32[128,512]{1,0:T(8,128)S(1)}, u32[]{:S(2)}, u32[]{:S(2)}) %collective-permute-start.14) | collective-permute-done | bytes 262176 | tf_op jit(solution)/shard_map/ppermute | solution.py:10
  982.8 11.6 %collective-permute-done.15 = f32[128,512]{1,0:T(8,128)S(1)} collective-permute-done((f32[128,512]{1,0:T(8,128)S(1)}, f32[128,512]{1,0:T(8,128)S(1)}, u32[]{:S(2)}, u32[]{:S(2)}) %collective-permute-start.15) | collective-permute-done | bytes 262176 | tf_op jit(solution)/shard_map/ppermute | solution.py:10
  (238 shorter events, 328.1 us)
Async XLA Ops:
  6.5 446.7 %all-reduce.7.cloned.1.call-start = ((), (), s32[]{:S(2)}) async-start(), calls=%async_computation.1 | async-start | bytes 1572864 | tf_op jit(solution)/shard_map/psum | solution.py:15
  47.1 20.7 %collective-permute-start = (f32[128,128]{1,0:T(8,128)S(1)}, f32[128,128]{1,0:T(8,128)S(1)}, u32[]{:S(2)}, u32[]{:S(2)}) collective-permute-start(f32[128,128]{1,0:T(8,128)S(1)} %fusion.141), channel_id=1, source_target_pairs={{0,32},{32,0},{64,96},{96,64},{128,160},{160,128},{192,224},{224,1... | collective-permute-start | bytes 196616 | tf_op jit(solution)/shard_map/ppermute | solution.py:10
  127.6 5.5 collective-permute-start.1
  182.2 7.9 collective-permute-start.2
  239.1 8.9 collective-permute-start.3
  295.3 157.9 %copy-start = (f32[512,512]{1,0:T(8,128)S(1)}, f32[512,512]{1,0:T(8,128)}, u32[]{:S(2)}) copy-start(f32[512,512]{1,0:T(8,128)} %param.6) | copy-start | bytes 3145732
  296.5 640.9 %all-reduce.5.cloned.1.call-start = ((), (), s32[]{:S(2)}) async-start(), calls=%async_computation | async-start | bytes 1572864 | tf_op jit(solution)/shard_map/psum | solution.py:15
  454.9 8.7 copy-start.1
  454.9 8.6 collective-permute-start.4
  464.0 9.4 collective-permute-start.5
  473.9 15.7 %collective-permute-start.6 = (f32[128,512]{1,0:T(8,128)S(1)}, f32[128,512]{1,0:T(8,128)S(1)}, u32[]{:S(2)}, u32[]{:S(2)}) collective-permute-start(f32[128,512]{1,0:T(8,128)S(1)} %fusion.4), channel_id=1, source_target_pairs={{0,128},{32,160},{64,192},{96,224},{128,0},{160,32},{192,64},{224,... | collective-permute-start | bytes 786440 | tf_op jit(solution)/shard_map/ppermute | solution.py:10
  490.0 20.1 %collective-permute-start.7 = (f32[128,512]{1,0:T(8,128)S(1)}, f32[128,512]{1,0:T(8,128)S(1)}, u32[]{:S(2)}, u32[]{:S(2)}) collective-permute-start(f32[128,512]{1,0:T(8,128)S(1)} %fusion.8), channel_id=1, source_target_pairs={{0,256},{32,288},{64,320},{96,352},{128,384},{160,416},{192,448},{... | collective-permute-start | bytes 786440 | tf_op jit(solution)/shard_map/ppermute | solution.py:10
  512.0 1.0 copy-start.2
  553.5 14.2 %collective-permute-start.8 = (f32[128,128]{1,0:T(8,128)S(1)}, f32[128,128]{1,0:T(8,128)S(1)}, u32[]{:S(2)}, u32[]{:S(2)}) collective-permute-start(f32[128,128]{1,0:T(8,128)S(1)} %fusion.146), channel_id=1, source_target_pairs={{0,32},{32,0},{64,96},{96,64},{128,160},{160,128},{192,224},{224,1... | collective-permute-start | bytes 196616 | tf_op jit(solution)/shard_map/ppermute | solution.py:10
  616.8 5.5 collective-permute-start.9
  671.2 7.8 collective-permute-start.10
  727.9 9.9 collective-permute-start.11
  939.1 8.7 copy-start.3
  939.1 8.6 collective-permute-start.12
  948.2 9.4 collective-permute-start.13
  958.1 15.7 %collective-permute-start.14 = (f32[128,512]{1,0:T(8,128)S(1)}, f32[128,512]{1,0:T(8,128)S(1)}, u32[]{:S(2)}, u32[]{:S(2)}) collective-permute-start(f32[128,512]{1,0:T(8,128)S(1)} %fusion.20), channel_id=1, source_target_pairs={{0,128},{32,160},{64,192},{96,224},{128,0},{160,32},{192,64},{224,... | collective-permute-start | bytes 786440 | tf_op jit(solution)/shard_map/ppermute | solution.py:10
  974.2 20.1 %collective-permute-start.15 = (f32[128,512]{1,0:T(8,128)S(1)}, f32[128,512]{1,0:T(8,128)S(1)}, u32[]{:S(2)}, u32[]{:S(2)}) collective-permute-start(f32[128,512]{1,0:T(8,128)S(1)} %fusion.24), channel_id=1, source_target_pairs={{0,256},{32,288},{64,320},{96,352},{128,384},{160,416},{192,448},{... | collective-permute-start | bytes 786440 | tf_op jit(solution)/shard_map/ppermute | solution.py:10
Sparse Core Ops, SparseCore 0:
  296.6 156.5 all-reduce.6
  786.3 151.0 all-reduce.4
where the time goes:
time: 1010 us; the launch traced here: 1000 us
  other arithmetic  474 us (47%)
  waiting for transfers between devices  395 us (39%)
  starting transfers between devices  76.4 us (8%)
  matrix products  39.8 us (4%)
  between operations  15.2 us (2%)
    psum x2, waiting for transfers between devices, spread_2(): return lax.psum(block, axis)  308 us
    another operation x30, other arithmetic, factor(): second_low = jnp.linalg.cholesky(outer_rows(basis_one, basis_one))  136 us
    another operation x30, other arithmetic, factor(): first_low = jnp.linalg.cholesky(contract_rows(columns, columns))  124 us
    another operation x20, other arithmetic, factor(): jax.scipy.linalg.solve_triangular(second_low, basis_one, lower=True)  106 us
    another operation x20, other arithmetic, factor(): jax.scipy.linalg.solve_triangular(first_low, columns.T, lower=True)  105 us
    ppermute x16, waiting for transfers between devices, swapped(): lax.ppermute(shard, axis, [(i, i ^ 1 << distance) for i in range(lax.axis...  87 us
    ppermute x16, starting transfers between devices, swapped(): lax.ppermute(shard, axis, [(i, i ^ 1 << distance) for i in range(lax.axis...  76.3 us
  transfers between devices with their start and end apart: 18, of which 16 were waited for; matrix products, arithmetic and copies ran while one was open for 2% of the time, Pallas kernels for 0%

commit v1 on v0

v1 whole, which is shorter than its diff:
```python
import jax
import jax.numpy as jnp
from jax import lax
from jax.experimental import pallas as pl
from jax.experimental.pallas import tpu as pltpu
from jax.sharding import PartitionSpec as P

PANEL = 128
LEAD = 2 * PANEL
LEAF = 64
SUB = 8
HI = lax.Precision.HIGHEST


def dot(left, right, dims):
    return lax.dot_general(left, right, (dims, ((), ())), precision=HI, preferred_element_type=jnp.float32)


NN = ((1,), (0,))
NT = ((1,), (1,))
TN = ((0,), (0,))


def leaf_inverse(block):
    groups = LEAF // SUB
    sub = lax.broadcasted_iota(jnp.int32, (SUB, 128), 0)

    def step(g, rows):
        rows = list(rows)
        live = [None] + [(q < groups - g) for q in range(1, groups)]
        cols = [[jnp.broadcast_to(rows[q][:, i:i + 1], (SUB, 128)) for i in range(SUB)] for q in range(groups)]
        pivots = jnp.ones((SUB, 128), jnp.float32)
        for i in range(SUB):
            pivots = jnp.where(sub == i, cols[0][i], pivots)
            inv = 1.0 / jnp.broadcast_to(cols[0][i][i:i + 1], (SUB, 128))
            line = jnp.broadcast_to(rows[0][i:i + 1], (SUB, 128)) * inv
            heads = [None] * SUB
            for j in range(i + 1, SUB):
                heads[j] = jnp.broadcast_to(cols[0][j][i:i + 1], (SUB, 128)) * inv
            for q in range(groups):
                keep = sub > i if q == 0 else live[q]
                mult = jnp.where(keep, cols[q][i], 0.0)
                rows[q] = rows[q] - mult * line
                for j in range(i + 1, SUB):
                    cols[q][j] = cols[q][j] - mult * heads[j]
        scale = lax.rsqrt(pivots)
        scale = scale * (1.5 - 0.5 * pivots * scale * scale)
        rows[0] = rows[0] * scale
        rows = rows[1:] + rows[:1]
        return tuple(pltpu.roll(r, 128 - SUB, 1) for r in rows)

    rows = tuple(block[q * SUB:(q + 1) * SUB] for q in range(groups))
    rows = lax.fori_loop(0, groups, step, rows)
    return jnp.concatenate(rows, axis=0)[:, :LEAF]


def chol_inverse(gram_ref, inv_ref, leaf_ref):
    inv_ref[...] = jnp.zeros_like(inv_ref)
    for b in range(LEAD // LEAF):
        at = pl.ds(b * LEAF, LEAF)
        strip = gram_ref[at, :]
        r = lax.broadcasted_iota(jnp.int32, (LEAF, LEAD), 0)
        c = lax.broadcasted_iota(jnp.int32, (LEAF, LEAD), 1)
        unit = jnp.where(c == r + b * LEAF, 1.0, 0.0).astype(jnp.float32)
        schur = dot(strip, unit, NT)
        rest = unit
        if b:
            done = inv_ref[...]
            low = dot(strip, done, NT)
            schur = schur - dot(low, low, NT)
            rest = unit - dot(low, done, NN)
        r = lax.broadcasted_iota(jnp.int32, (LEAF, 2 * LEAF), 0)
        c = lax.broadcasted_iota(jnp.int32, (LEAF, 2 * LEAF), 1)
        leaf_ref[...] = jnp.where(c == r + LEAF, 1.0, 0.0).astype(jnp.float32)
        leaf_ref[:, :LEAF] = schur
        leaf = leaf_inverse(leaf_ref[...])
        inv_ref[at, :] = dot(leaf, rest, NN)


def chol_inv_call(gram):
    return pl.pallas_call(
        chol_inverse,
        out_shape=jax.ShapeDtypeStruct((LEAD, LEAD), jnp.float32),
        scratch_shapes=[pltpu.VMEM((LEAF, 2 * LEAF), jnp.float32)],
    )(gram)


def local(panels):
    me = lax.axis_index("col")
    head = panels[:, :PANEL]
    zero = jnp.zeros_like(head)
    lead = lax.psum(
        jnp.concatenate([jnp.where(me == 0, head, zero), jnp.where(me == 1, head, zero)], axis=1), "col")
    gram = lax.psum(dot(lead, lead, TN), "row")
    cross = lax.psum(dot(lead, panels, TN), "row")
    inv_one = chol_inv_call(gram)
    basis = dot(inv_one, lead, NT)
    inv_two = chol_inv_call(lax.psum(dot(basis, basis, NT), "row"))
    top = dot(inv_two, dot(inv_one, cross, NN), NN)
    col_iota = jnp.arange(panels.shape[1], dtype=jnp.int32)
    global_col = (col_iota // PANEL * lax.axis_size("col") + me) * PANEL + col_iota % PANEL
    row_iota = jnp.arange(LEAD, dtype=jnp.int32)
    return jnp.where(global_col[None, :] >= row_iota[:, None], top, jnp.zeros_like(top))


def solution(mesh):
    return jax.shard_map(local, mesh=mesh, in_specs=(P("row", "col"),), out_specs=P(None, "col"), check_vma=False)
```

time: 1010 us -> 454 us (0.45)
  other arithmetic: 474 us -> 1.82 us
  starting transfers between devices: 76.4 us -> 0.09 us
  Pallas kernels: 0 us -> 29.7 us
  matrix products: 39.8 us -> 11.7 us
    another operation x100 -> x0, other arithmetic: 471 us -> none  [the longest x30 136 us: factor(): second_low = jnp.linalg.cholesky(outer_rows(basis_one, basis_one))]
    psum x2 -> x3, waiting for transfers between devices: 308 us -> 397 us  [the longest x1 163 us: local(): lax.psum(jnp.concatenate([jnp.where(me == 0, head, zero), jnp.where(me ==...]
    ppermute x16 -> x0, waiting for transfers between devices: 87 us -> none  [swapped(): lax.ppermute(shard, axis, [(i, i ^ 1 << distance) for i in range(lax.axis...]
    ppermute x16 -> x0, starting transfers between devices: 76.3 us -> none  [swapped(): lax.ppermute(shard, axis, [(i, i ^ 1 << distance) for i in range(lax.axis...]
    pallas_call x0 -> x2, Pallas kernels: none -> 29.7 us  [chol_inv_call(): pl.pallas_call(chol_inverse, out_shape=jax.ShapeDtypeStruct((LEAD, LEAD),...]
    dot_general x43 -> x6, matrix products: 30.7 us -> 11.7 us  [dot(): lax.dot_general(left, right, (dims, ((), ())), precision=HI, preferred_el...]
  transfers between devices with their start and end apart: 18 -> 3, of which waited for: 16 -> 3; matrix products, arithmetic and copies ran while one was open for 2% -> 0% of each run, Pallas kernels for 0% -> 0%
where the time goes in v1:
time: 454 us
  waiting for transfers between devices  397 us (87%)
  Pallas kernels  29.7 us (7%)
  between operations  13.2 us (3%)
  matrix products  11.7 us (3%)
    psum x1, waiting for transfers between devices, local(): lax.psum(jnp.concatenate([jnp.where(me == 0, head, zero), jnp.where(me ==...  163 us
    psum x1, waiting for transfers between devices, local(): inv_two = chol_inv_call(lax.psum(dot(basis, basis, NT), 'row'))  118 us
    psum x1, waiting for transfers between devices, local(): gram = lax.psum(dot(lead, lead, TN), 'row')  116 us
    pallas_call x2, Pallas kernels, chol_inv_call(): pl.pallas_call(chol_inverse, out_shape=jax.ShapeDtypeStruct((LEAD, LEAD),...  29.7 us
    dot_general x6, matrix products, dot(): lax.dot_general(left, right, (dims, ((), ())), precision=HI, preferred_el...  11.7 us
  transfers between devices with their start and end apart: 3, of which 3 were waited for; matrix products, arithmetic and copies ran while one was open for 0% of the time, Pallas kernels for 0%

profile of v1, /device:TPU:1, one launch (start us, length us, event | category | flops | bytes accessed | tf_op | source)
XLA Modules:
  0.0 453.7 jit_solution(5749378173332876706)
XLA Ops:
  6.5 0.0 all-reduce.5.cloned.1.call-start
  6.5 1.0 slice_select_fusion.1
  7.5 0.8 pad_maximum_fusion
  8.4 0.0 copy-start.2
  8.4 0.0 all-reduce.5.cloned.1.call-update
  8.4 0.0 all-reduce.7.cloned.1.call-start
  8.4 162.8 %all-reduce.5.cloned.1.call-done = f32[512,256]{1,0:T(8,128)} async-done(((f32[512,256]{1,0:T(8,128)}), f32[512,256]{1,0:T(8,128)}) %all-reduce.5.cloned.1.call-update) | async-done | bytes 524304 | tf_op jit(solution)/shard_map/psum | solution.py:92
  171.3 0.0 copy-start
  171.3 3.0 fusion.11
  174.2 0.0 all-reduce.7.cloned.1.call-update
  174.2 0.0 all-reduce.9.cloned.1.call-start
  174.3 0.0 copy-done.2
  174.3 0.0 copy-done
  174.3 1.9 fusion.14
  176.2 116.4 %all-reduce.7.cloned.1.call-done.gram_ref = f32[256,256]{1,0:T(8,128)} async-done(((f32[256,256]{1,0:T(8,128)}), f32[256,256]{1,0:T(8,128)}) %all-reduce.7.cloned.1.call-update) | async-done | bytes 262160 | tf_op jit(solution)/shard_map/psum | solution.py:94
  292.5 14.8 %shard_map.17 = f32[256,256]{1,0:T(8,128)} custom-call(f32[256,256]{1,0:T(8,128)} %all-reduce.7.cloned.1.call-done.gram_ref), custom_call_target="tpu_custom_call" | custom-call | tf_op jit(solution)/shard_map/pallas_call | solution.py:81
  307.4 1.6 fusion.12
  309.0 1.3 fusion.13
  310.3 0.0 copy-start.1
  310.3 0.0 all-reduce.9.cloned.1.call-update
  310.3 118.0 %all-reduce.9.cloned.1.call-done = (f32[256,256]{1,0:T(8,128)}, f32[256,512]{1,0:T(8,128)}) async-done(((f32[256,256]{1,0:T(8,128)}, f32[256,512]{1,0:T(8,128)}), (f32[256,256]{1,0:T(8,128)}, f32[256,512]{1,0:T(8,128)})) %all-reduce.9.cloned.1.call-update) | async-done | bytes 786448 | tf_op jit(solution)/shard_map/psum | solution.py:98
  428.3 0.0 copy-done.1
  428.3 1.7 fusion.15
  430.0 14.8 %shard_map.18 = f32[256,256]{1,0:T(8,128)} custom-call(f32[256,256]{1,0:T(8,128)} %get-tuple-element.5.gram_ref), custom_call_target="tpu_custom_call" | custom-call | tf_op jit(solution)/shard_map/pallas_call | solution.py:81
  444.8 2.4 convolution_select_fusion
  (1 shorter events, 0.0 us)
Async XLA Ops:
  6.5 164.7 %all-reduce.5.cloned.1.call-start = ((), (), s32[]{:S(2)}) async-start(), calls=%async_computation | async-start | bytes 1048576 | tf_op jit(solution)/shard_map/psum | solution.py:92
  8.4 165.9 %copy-start.2 = (f32[512,512]{1,0:T(8,128)S(1)}, f32[512,512]{1,0:T(8,128)}, u32[]{:S(2)}) copy-start(f32[512,512]{1,0:T(8,128)} %param.1) | copy-start | bytes 3145732
  8.4 284.2 %all-reduce.7.cloned.1.call-start = ((), (), s32[]{:S(2)}) async-start(), calls=%async_computation.1 | async-start | bytes 524288 | tf_op jit(solution)/shard_map/psum | solution.py:94
  171.3 3.1 copy-start
  174.2 254.0 %all-reduce.9.cloned.1.call-start = ((), (), s32[]{:S(2)}) async-start(), calls=%async_computation.2 | async-start | bytes 1572864 | tf_op jit(solution)/shard_map/psum | solution.py:98
  310.3 118.0 %copy-start.1 = (f32[256,256]{1,0:T(8,128)S(1)}, f32[256,256]{1,0:T(8,128)}, u32[]{:S(2)}) copy-start(f32[256,256]{1,0:T(8,128)} %shard_map.17) | copy-start | bytes 786436
Sparse Core Ops, SparseCore 0:
  10.7 160.4 all-reduce.4
  174.4 118.1 all-reduce.6
  310.4 117.8 all-reduce.8

commit v2 on v1

--- a/solution.py
+++ b/solution.py
@@ -8,6 +8,12 @@
 PANEL = 128
 LEAD = 2 * PANEL
 LEAF = 64
+X_SIZE = 4
+Y_SIZE = 8
+N_ROW = 16
+N_Z = 8
+CHUNKS = 4
+MESH = pl.DeviceIdType.MESH
 SUB = 8
 HI = lax.Precision.HIGHEST
 
@@ -54,8 +60,8 @@
     return jnp.concatenate(rows, axis=0)[:, :LEAF]
 
 
-def chol_inverse(gram_ref, inv_ref, leaf_ref):
-    inv_ref[...] = jnp.zeros_like(inv_ref)
+def chol_inverse(gram_ref, inv_ref, leaf_ref, between=()):
+    inv_ref[...] = jnp.zeros(inv_ref.shape, jnp.float32)
     for b in range(LEAD // LEAF):
         at = pl.ds(b * LEAF, LEAF)
         strip = gram_ref[at, :]
@@ -75,32 +81,249 @@
         leaf_ref[:, :LEAF] = schur
         leaf = leaf_inverse(leaf_ref[...])
         inv_ref[at, :] = dot(leaf, rest, NN)
-
-
-def chol_inv_call(gram):
+        if b < len(between):
+            between[b]()
+
+
+def far_first(count):
+    return sorted(range(1, count), key=lambda off: -min(off, count - off))
+
+
+def kernel(panels_ref, out_ref, lead_ref, part_ref, recv_ref, gram_ref, inv_ref, leaf_ref,
+           c_part, c_pair, c_half, c_recv, cross_ref,
+           bc_send, bc_recv, rs_send, rs_recv, ag_send, ag_recv,
+           pair_send, pair_recv, crs_send, crs_recv, cag_send, cag_recv):
+    me = lax.axis_index("row")
+    col = lax.axis_index("col")
+    core = lax.rem(me, 2)
+    z = me // 2
+    x = col // Y_SIZE
+    y = lax.rem(col, Y_SIZE)
+
+    def at_xy(dx, dy):
+        return {"col": lax.rem(x + dx + X_SIZE, X_SIZE) * Y_SIZE + lax.rem(y + dy + Y_SIZE, Y_SIZE)}
+
+    def row_peer(off):
+        return {"row": lax.rem(me + off, N_ROW)}
+
+    partner = {"row": z * 2 + 1 - core}
+    near = [at_xy(0, 1), at_xy(0, -1), at_xy(1, 0), at_xy(-1, 0)]
+
+    barrier = pltpu.get_barrier_semaphore()
+    for off in far_first(N_ROW):
+        pl.semaphore_signal(barrier, inc=1, device_id=row_peer(off), device_id_type=MESH)
+    for device in near:
+        pl.semaphore_signal(barrier, inc=1, device_id=device, device_id_type=MESH)
+    pl.semaphore_wait(barrier, N_ROW - 1 + len(near))
+
+    half_rows = lead_ref.shape[1] // 2
+    size = half_rows // CHUNKS
+
+    def sends(tree, panel):
+        d = lax.rem(y - panel + Y_SIZE, Y_SIZE)
+        up, down = d <= 3, (d == 0) | (d >= 6)
+        if tree == 0:
+            return [(x == 0) & up, (x == 0) & down, x <= 1, x == 0]
+        return [(x != 0) & up, (x != 0) & down, (d == 0) & (x <= 1),
+                ((d == 0) & (x == 0)) | ((d != 0) & (x == 1))]
+
+    def hop(k, tree, panel, way, own):
+        rows = pl.ds(pl.multiple_of(tree * half_rows + k * size, size), size)
+        piece = (k * 2 + tree) * 2 + panel
+        return pltpu.make_async_remote_copy(
+            src_ref=panels_ref.at[rows, pl.ds(0, PANEL)] if own else lead_ref.at[panel, rows],
+            dst_ref=lead_ref.at[panel, rows],
+            send_sem=bc_send.at[piece, way], recv_sem=bc_recv.at[piece],
+            device_id=near[way], device_id_type=MESH)
+
+    def pass_on(k, carry):
+        for tree in range(2):
+            for panel in range(2):
+                cond = sends(tree, panel)
+
+                @pl.when(col == panel)
+                def _():
+                    for way in range(4):
+                        @pl.when(cond[way])
+                        def _():
+                            hop(k, tree, panel, way, True).start()
+
+                @pl.when(col != panel)
+                def _():
+                    hop(k, tree, panel, 0, False).wait_recv()
+                    for way in range(4):
+                        @pl.when(cond[way])
+                        def _():
+                            hop(k, tree, panel, way, False).start()
+        return carry
+
+    lax.fori_loop(0, CHUNKS, pass_on, 0)
+    for panel in range(2):
+        @pl.when(col == panel)
+        def _():
+            lead_ref[panel] = panels_ref[:, :PANEL]
+
+    def lead():
+        return jnp.concatenate([lead_ref[0], lead_ref[1]], axis=1)
+
+    own_rows = N_ROW
+    mine = pl.ds(pl.multiple_of(me * own_rows, own_rows), own_rows)
+
+    def rs_copy(p, off):
+        peer = lax.rem(me + off, N_ROW)
+        return pltpu.make_async_remote_copy(
+            src_ref=part_ref.at[p, pl.ds(pl.multiple_of(peer * own_rows, own_rows), own_rows)],
+            dst_ref=recv_ref.at[p, off - 1],
+            send_sem=rs_send.at[p, off - 1], recv_sem=rs_recv.at[p, off - 1],
+            device_id=row_peer(off), device_id_type=MESH)
+
+    def ag_copy(p, off):
+        return pltpu.make_async_remote_copy(
+            src_ref=gram_ref.at[p, mine], dst_ref=gram_ref.at[p, mine],
+            send_sem=ag_send.at[p, off - 1], recv_sem=ag_recv.at[p, off - 1],
+            device_id=row_peer(off), device_id_type=MESH)
+
+    def scatter_start(p):
+        for off in far_first(N_ROW):
+            rs_copy(p, off).start()
+
+    def scatter_finish(p):
+        total = part_ref[p, mine]
+        for off in reversed(far_first(N_ROW)):
+            rs_copy(p, off).wait_recv()
+            total = total + recv_ref[p, off - 1]
+        gram_ref[p, mine] = total
+        for off in far_first(N_ROW):
+            ag_copy(p, off).start()
+
+    def gather_finish(p):
+        for off in reversed(far_first(N_ROW)):
+            ag_copy(p, off).wait_recv()
+
+    c_rows = LEAD // 2 // N_Z
+    keep = pl.ds(pl.multiple_of(core * PANEL, PANEL), PANEL)
+    give = pl.ds(pl.multiple_of((1 - core) * PANEL, PANEL), PANEL)
+    c_mine = pl.ds(pl.multiple_of(core * PANEL + z * c_rows, c_rows), c_rows)
+
+    def pair_copy(step):
+        return pltpu.make_async_remote_copy(
+            src_ref=cross_ref.at[keep] if step else c_part.at[give],
+            dst_ref=cross_ref.at[keep] if step else c_pair,
+            send_sem=pair_send.at[step], recv_sem=pair_recv.at[step],
+            device_id=partner, device_id_type=MESH)
+
+    def crs_copy(off):
+        peer_z = lax.rem(z + off, N_Z)
+        return pltpu.make_async_remote_copy(
+            src_ref=c_half.at[pl.ds(pl.multiple_of(peer_z * c_rows, c_rows), c_rows)],
+            dst_ref=c_recv.at[off - 1],
+            send_sem=crs_send.at[off - 1], recv_sem=crs_recv.at[off - 1],
+            device_id=row_peer(2 * off), device_id_type=MESH)
+
+    def cag_copy(off):
+        return pltpu.make_async_remote_copy(
+            src_ref=cross_ref.at[c_mine], dst_ref=cross_ref.at[c_mine],
+            send_sem=cag_send.at[off - 1], recv_sem=cag_recv.at[off - 1],
+            device_id=row_peer(2 * off), device_id_type=MESH)
+
+    def cross_scatter():
+        pair_copy(0).wait_recv()
+        c_half[...] = c_part[keep] + c_pair[...]
+        for off in far_first(N_Z):
+            crs_copy(off).start()
+
+    def cross_gather():
+        total = c_half[pl.ds(pl.multiple_of(z * c_rows, c_rows), c_rows)]
+        for off in reversed(far_first(N_Z)):
+            crs_copy(off).wait_recv()
+            total = total + c_recv[off - 1]
+        cross_ref[c_mine] = total
+        for off in far_first(N_Z):
+            cag_copy(off).start()
+
+    def cross_pair():
+        for off in far_first(N_Z):
+            cag_copy(off).wait_recv()
+        pair_copy(1).start()
+
+    part_ref[0] = dot(lead(), lead(), TN)
+    scatter_start(0)
+    c_part[...] = dot(lead(), panels_ref[...], TN)
+    pair_copy(0).start()
+    scatter_finish(0)
+    gather_finish(0)
+    cross_scatter()
+    chol_inverse(gram_ref.at[0], inv_ref.at[0], leaf_ref, (lambda: None, cross_gather))
+    basis = dot(inv_ref[0], lead(), NT)
+    part_ref[1] = dot(basis, basis, NT)
+    scatter_start(1)
+    cross_pair()
+    scatter_finish(1)
+    pair_copy(1).wait_recv()
+    c_part_done = [pair_copy(0), pair_copy(1)]
+    for copy in c_part_done:
+        copy.wait_send()
+    c_part[...] = dot(inv_ref[0], cross_ref[...], NN)
+    gather_finish(1)
+    chol_inverse(gram_ref.at[1], inv_ref.at[1], leaf_ref)
+    top = dot(inv_ref[1], c_part[...], NN)
+    width = out_ref.shape[1]
+    r = lax.broadcasted_iota(jnp.int32, (LEAD, width), 0)
+    c = lax.broadcasted_iota(jnp.int32, (LEAD, width), 1)
+    global_col = (c // PANEL * (X_SIZE * Y_SIZE) + col) * PANEL + lax.rem(c, PANEL)
+    out_ref[...] = jnp.where(global_col >= r, top, 0.0)
+
+    for p in range(2):
+        for off in range(1, N_ROW):
+            rs_copy(p, off).wait_send()
+            ag_copy(p, off).wait_send()
+    for off in range(1, N_Z):
+        crs_copy(off).wait_send()
+        cag_copy(off).wait_send()
+
+    def drain(k, carry):
+        for tree in range(2):
+            for panel in range(2):
+                cond = sends(tree, panel)
+                for way in range(4):
+                    @pl.when(cond[way])
+                    def _():
+                        hop(k, tree, panel, way, False).wait_send()
+        return carry
+
+    lax.fori_loop(0, CHUNKS, drain, 0)
+
+
+def local(panels):
+    rows, width = panels.shape
+    f32 = jnp.float32
+    vmem, dma = pltpu.VMEM, pltpu.SemaphoreType.DMA
     return pl.pallas_call(
-        chol_inverse,
-        out_shape=jax.ShapeDtypeStruct((LEAD, LEAD), jnp.float32),
-        scratch_shapes=[pltpu.VMEM((LEAF, 2 * LEAF), jnp.float32)],
-    )(gram)
-
-
-def local(panels):
-    me = lax.axis_index("col")
-    head = panels[:, :PANEL]
-    zero = jnp.zeros_like(head)
-    lead = lax.psum(
-        jnp.concatenate([jnp.where(me == 0, head, zero), jnp.where(me == 1, head, zero)], axis=1), "col")
-    gram = lax.psum(dot(lead, lead, TN), "row")
-    cross = lax.psum(dot(lead, panels, TN), "row")
-    inv_one = chol_inv_call(gram)
-    basis = dot(inv_one, lead, NT)
-    inv_two = chol_inv_call(lax.psum(dot(basis, basis, NT), "row"))
-    top = dot(inv_two, dot(inv_one, cross, NN), NN)
-    col_iota = jnp.arange(panels.shape[1], dtype=jnp.int32)
-    global_col = (col_iota // PANEL * lax.axis_size("col") + me) * PANEL + col_iota % PANEL
-    row_iota = jnp.arange(LEAD, dtype=jnp.int32)
-    return jnp.where(global_col[None, :] >= row_iota[:, None], top, jnp.zeros_like(top))
+        kernel,
+        out_shape=jax.ShapeDtypeStruct((LEAD, width), f32),
+        in_specs=[pl.BlockSpec(memory_space=vmem)],
+        out_specs=pl.BlockSpec(memory_space=vmem),
+        scratch_shapes=[
+            vmem((2, rows, PANEL), f32),
+            vmem((2, LEAD, LEAD), f32),
+            vmem((2, N_ROW - 1, N_ROW, LEAD), f32),
+            vmem((2, LEAD, LEAD), f32),
+            vmem((2, LEAD, LEAD), f32),
+            vmem((LEAF, 2 * LEAF), f32),
+            vmem((LEAD, width), f32),
+            vmem((PANEL, width), f32),
+            vmem((PANEL, width), f32),
+            vmem((N_Z - 1, LEAD // 2 // N_Z, width), f32),
+            vmem((LEAD, width), f32),
+            dma((CHUNKS * 4, 4)), dma((CHUNKS * 4,)),
+            dma((2, N_ROW - 1)), dma((2, N_ROW - 1)),
+            dma((2, N_ROW - 1)), dma((2, N_ROW - 1)),
+            dma((2,)), dma((2,)),
+            dma((N_Z - 1,)), dma((N_Z - 1,)),
+            dma((N_Z - 1,)), dma((N_Z - 1,)),
+        ],
+        compiler_params=pltpu.CompilerParams(collective_id=0, has_side_effects=True),
+    )(panels)
 
 
 def solution(mesh):

time: 454 us -> 180 us (0.40)
  the two profiles are of different devices: /device:TPU:1 before, /device:TPU:41 now
where the time goes in v2:
time: 180 us
  Pallas kernels  178 us (99%)
  local copies, waits for them, and re-layouts  1.87 us (1%)
    pallas_call x1, Pallas kernels, local(): pl.pallas_call(kernel, out_shape=jax.ShapeDtypeStruct((LEAD, width), f32)...  178 us

profile of v2, /device:TPU:41, one launch (start us, length us, event | category | flops | bytes accessed | tf_op | source)
XLA Modules:
  0.0 179.5 jit_solution(18350580560174103876)
XLA Ops:
  0.0 177.7 %shard_map.17 = f32[256,512]{1,0:T(8,128)} custom-call(f32[512,512]{1,0:T(8,128)} %panels_ref.1), custom_call_target="tpu_custom_call" | custom-call | tf_op jit(solution)/shard_map/pallas_call | solution.py:301
  177.7 1.9 %copy.3 = f32[256,512]{1,0:T(8,128)} copy(f32[256,512]{1,0:T(8,128)} %shard_map.17) | data formatting | bytes 1048576

commit v3 on v2

--- a/solution.py
+++ b/solution.py
@@ -127,6 +127,9 @@
         return [(x != 0) & up, (x != 0) & down, (d == 0) & (x <= 1),
                 ((d == 0) & (x == 0)) | ((d != 0) & (x == 1))]
 
+    def relays(cond):
+        return cond[0] | cond[1] | cond[2] | cond[3]
+
     def hop(k, tree, panel, way, own):
         rows = pl.ds(pl.multiple_of(tree * half_rows + k * size, size), size)
         piece = (k * 2 + tree) * 2 + panel
@@ -148,7 +151,7 @@
                         def _():
                             hop(k, tree, panel, way, True).start()
 
-                @pl.when(col != panel)
+                @pl.when((col != panel) & relays(cond))
                 def _():
                     hop(k, tree, panel, 0, False).wait_recv()
                     for way in range(4):
@@ -157,7 +160,16 @@
                             hop(k, tree, panel, way, False).start()
         return carry
 
+    def take_last(k, carry):
+        for tree in range(2):
+            for panel in range(2):
+                @pl.when((col != panel) & jnp.logical_not(relays(sends(tree, panel))))
+                def _():
+                    hop(k, tree, panel, 0, False).wait_recv()
+        return carry
+
     lax.fori_loop(0, CHUNKS, pass_on, 0)
+    lax.fori_loop(0, CHUNKS, take_last, 0)
     for panel in range(2):
         @pl.when(col == panel)
         def _():

time: 180 us -> 122 us (0.68)
  the two profiles are of different devices: /device:TPU:41 before, /device:TPU:45 now
where the time goes in v3:
time: 122 us
  Pallas kernels  120 us (98%)
  local copies, waits for them, and re-layouts  1.87 us (2%)
    pallas_call x1, Pallas kernels, local(): pl.pallas_call(kernel, out_shape=jax.ShapeDtypeStruct((LEAD, width), f32)...  120 us

profile of v3, /device:TPU:45, one launch (start us, length us, event | category | flops | bytes accessed | tf_op | source)
XLA Modules:
  0.0 121.5 jit_solution(12778942393275655844)
XLA Ops:
  0.0 119.7 %shard_map.17 = f32[256,512]{1,0:T(8,128)} custom-call(f32[512,512]{1,0:T(8,128)} %panels_ref.1), custom_call_target="tpu_custom_call" | custom-call | tf_op jit(solution)/shard_map/pallas_call | solution.py:313
  119.7 1.9 %copy.3 = f32[256,512]{1,0:T(8,128)} copy(f32[256,512]{1,0:T(8,128)} %shard_map.17) | data formatting | bytes 1048576

commit v4 on v3

--- a/solution.py
+++ b/solution.py
@@ -12,7 +12,7 @@
 Y_SIZE = 8
 N_ROW = 16
 N_Z = 8
-CHUNKS = 4
+CHUNKS = 2
 MESH = pl.DeviceIdType.MESH
 SUB = 8
 HI = lax.Precision.HIGHEST
@@ -57,39 +57,42 @@
 
     rows = tuple(block[q * SUB:(q + 1) * SUB] for q in range(groups))
     rows = lax.fori_loop(0, groups, step, rows)
-    return jnp.concatenate(rows, axis=0)[:, :LEAF]
-
-
-def chol_inverse(gram_ref, inv_ref, leaf_ref, between=()):
-    inv_ref[...] = jnp.zeros(inv_ref.shape, jnp.float32)
-    for b in range(LEAD // LEAF):
-        at = pl.ds(b * LEAF, LEAF)
-        strip = gram_ref[at, :]
-        r = lax.broadcasted_iota(jnp.int32, (LEAF, LEAD), 0)
-        c = lax.broadcasted_iota(jnp.int32, (LEAF, LEAD), 1)
-        unit = jnp.where(c == r + b * LEAF, 1.0, 0.0).astype(jnp.float32)
-        schur = dot(strip, unit, NT)
-        rest = unit
-        if b:
-            done = inv_ref[...]
-            low = dot(strip, done, NT)
-            schur = schur - dot(low, low, NT)
-            rest = unit - dot(low, done, NN)
-        r = lax.broadcasted_iota(jnp.int32, (LEAF, 2 * LEAF), 0)
-        c = lax.broadcasted_iota(jnp.int32, (LEAF, 2 * LEAF), 1)
-        leaf_ref[...] = jnp.where(c == r + LEAF, 1.0, 0.0).astype(jnp.float32)
-        leaf_ref[:, :LEAF] = schur
-        leaf = leaf_inverse(leaf_ref[...])
-        inv_ref[at, :] = dot(leaf, rest, NN)
-        if b < len(between):
-            between[b]()
+    rows = jnp.concatenate(rows, axis=0)
+    return jnp.where(lax.broadcasted_iota(jnp.int32, rows.shape, 1) < LEAF, rows, 0.0)
+
+
+def panel_inverse(block):
+    r = lax.broadcasted_iota(jnp.int32, (LEAF, PANEL), 0)
+    c = lax.broadcasted_iota(jnp.int32, (LEAF, PANEL), 1)
+    unit = jnp.where(c == r + LEAF, 1.0, 0.0).astype(jnp.float32)
+    none = jnp.zeros((LEAF, PANEL), jnp.float32)
+    first = leaf_inverse(jnp.where(c < LEAF, block[:LEAF], unit))
+    above = jnp.concatenate([first, none], axis=0)
+    low = dot(block[LEAF:], above, NT)
+    schur = block[LEAF:] - dot(low, jnp.concatenate([none, low], axis=0), NT)
+    rest = unit - dot(low, above, NN)
+    second = leaf_inverse(jnp.where(c < LEAF, pltpu.roll(schur, LEAF, 1), unit))
+    return jnp.concatenate([first, dot(second, jnp.concatenate([rest, none], axis=0), NN)], axis=0)
+
+
+def chol_inverse(gram_ref, inv_ref, between=lambda: None):
+    first = panel_inverse(gram_ref[:PANEL, :PANEL])
+    low = dot(gram_ref[PANEL:, :PANEL], first, NT)
+    schur = gram_ref[PANEL:, PANEL:] - dot(low, low, NT)
+    inv_ref[:PANEL, :PANEL] = first
+    inv_ref[:PANEL, PANEL:] = jnp.zeros((PANEL, PANEL), jnp.float32)
+    between()
+    rest = dot(low, first, NN)
+    second = panel_inverse(schur)
+    inv_ref[PANEL:, PANEL:] = second
+    inv_ref[PANEL:, :PANEL] = -dot(second, rest, NN)
 
 
 def far_first(count):
     return sorted(range(1, count), key=lambda off: -min(off, count - off))
 
 
-def kernel(panels_ref, out_ref, lead_ref, part_ref, recv_ref, gram_ref, inv_ref, leaf_ref,
+def kernel(panels_ref, out_ref, lead_ref, part_ref, recv_ref, gram_ref, inv_ref,
            c_part, c_pair, c_half, c_recv, cross_ref,
            bc_send, bc_recv, rs_send, rs_recv, ag_send, ag_recv,
            pair_send, pair_recv, crs_send, crs_recv, cag_send, cag_recv):
@@ -139,17 +142,22 @@
             send_sem=bc_send.at[piece, way], recv_sem=bc_recv.at[piece],
             device_id=near[way], device_id_type=MESH)
 
+    def send_own(k, carry):
+        for panel in range(2):
+            @pl.when(col == panel)
+            def _():
+                for tree in range(2):
+                    cond = sends(tree, panel)
+                    for way in range(4):
+                        @pl.when(cond[way])
+                        def _():
+                            hop(k, tree, panel, way, True).start()
+        return carry
+
     def pass_on(k, carry):
         for tree in range(2):
             for panel in range(2):
                 cond = sends(tree, panel)
-
-                @pl.when(col == panel)
-                def _():
-                    for way in range(4):
-                        @pl.when(cond[way])
-                        def _():
-                            hop(k, tree, panel, way, True).start()
 
                 @pl.when((col != panel) & relays(cond))
                 def _():
@@ -168,6 +176,7 @@
                     hop(k, tree, panel, 0, False).wait_recv()
         return carry
 
+    lax.fori_loop(0, CHUNKS, send_own, 0)
     lax.fori_loop(0, CHUNKS, pass_on, 0)
     lax.fori_loop(0, CHUNKS, take_last, 0)
     for panel in range(2):
@@ -265,7 +274,7 @@
     scatter_finish(0)
     gather_finish(0)
     cross_scatter()
-    chol_inverse(gram_ref.at[0], inv_ref.at[0], leaf_ref, (lambda: None, cross_gather))
+    chol_inverse(gram_ref.at[0], inv_ref.at[0], cross_gather)
     basis = dot(inv_ref[0], lead(), NT)
     part_ref[1] = dot(basis, basis, NT)
     scatter_start(1)
@@ -277,7 +286,7 @@
         copy.wait_send()
     c_part[...] = dot(inv_ref[0], cross_ref[...], NN)
     gather_finish(1)
-    chol_inverse(gram_ref.at[1], inv_ref.at[1], leaf_ref)
+    chol_inverse(gram_ref.at[1], inv_ref.at[1])
     top = dot(inv_ref[1], c_part[...], NN)
     width = out_ref.shape[1]
     r = lax.broadcasted_iota(jnp.int32, (LEAD, width), 0)
@@ -321,7 +330,6 @@
             vmem((2, N_ROW - 1, N_ROW, LEAD), f32),
             vmem((2, LEAD, LEAD), f32),
             vmem((2, LEAD, LEAD), f32),
-            vmem((LEAF, 2 * LEAF), f32),
             vmem((LEAD, width), f32),
             vmem((PANEL, width), f32),
             vmem((PANEL, width), f32),

time: 122 us -> 110 us (0.902)
  Pallas kernels: 120 us -> 108 us
    pallas_call x1, Pallas kernels: 120 us -> 108 us  [local(): pl.pallas_call(kernel, out_shape=jax.ShapeDtypeStruct((LEAD, width), f32)...]
where the time goes in v4:
time: 110 us
  Pallas kernels  108 us (98%)
  local copies, waits for them, and re-layouts  1.87 us (2%)
    pallas_call x1, Pallas kernels, local(): pl.pallas_call(kernel, out_shape=jax.ShapeDtypeStruct((LEAD, width), f32)...  108 us

profile of v4, /device:TPU:45, one launch (start us, length us, event | category | flops | bytes accessed | tf_op | source)
XLA Modules:
  0.0 109.9 jit_solution(2612469384329213380)
XLA Ops:
  0.0 108.1 %shard_map.17 = f32[256,512]{1,0:T(8,128)} custom-call(f32[512,512]{1,0:T(8,128)} %panels_ref.1), custom_call_target="tpu_custom_call" | custom-call | tf_op jit(solution)/shard_map/pallas_call | solution.py:322
  108.1 1.9 %copy.3 = f32[256,512]{1,0:T(8,128)} copy(f32[256,512]{1,0:T(8,128)} %shard_map.17) | data formatting | bytes 1048576

commit v5 on v4

--- a/solution.py
+++ b/solution.py
@@ -8,11 +8,12 @@
 PANEL = 128
 LEAD = 2 * PANEL
 LEAF = 64
+GRAM = 3 * PANEL
 X_SIZE = 4
 Y_SIZE = 8
 N_ROW = 16
 N_Z = 8
-CHUNKS = 2
+CHUNKS = 1
 MESH = pl.DeviceIdType.MESH
 SUB = 8
 HI = lax.Precision.HIGHEST
@@ -76,9 +77,9 @@
 
 
 def chol_inverse(gram_ref, inv_ref, between=lambda: None):
-    first = panel_inverse(gram_ref[:PANEL, :PANEL])
-    low = dot(gram_ref[PANEL:, :PANEL], first, NT)
-    schur = gram_ref[PANEL:, PANEL:] - dot(low, low, NT)
+    first = panel_inverse(gram_ref[:PANEL])
+    low = dot(gram_ref[PANEL:2 * PANEL], first, NT)
+    schur = gram_ref[2 * PANEL:] - dot(low, low, NT)
     inv_ref[:PANEL, :PANEL] = first
     inv_ref[:PANEL, PANEL:] = jnp.zeros((PANEL, PANEL), jnp.float32)
     between()
@@ -187,7 +188,7 @@
     def lead():
         return jnp.concatenate([lead_ref[0], lead_ref[1]], axis=1)
 
-    own_rows = N_ROW
+    own_rows = GRAM // N_ROW
     mine = pl.ds(pl.multiple_of(me * own_rows, own_rows), own_rows)
 
     def rs_copy(p, off):
@@ -203,6 +204,11 @@
             src_ref=gram_ref.at[p, mine], dst_ref=gram_ref.at[p, mine],
             send_sem=ag_send.at[p, off - 1], recv_sem=ag_recv.at[p, off - 1],
             device_id=row_peer(off), device_id_type=MESH)
+
+    def gram_blocks(p, left, right, dims):
+        part_ref[p, :PANEL] = dot(left, left, dims)
+        part_ref[p, PANEL:2 * PANEL] = dot(right, left, dims)
+        part_ref[p, 2 * PANEL:] = dot(right, right, dims)
 
     def scatter_start(p):
         for off in far_first(N_ROW):
@@ -267,7 +273,7 @@
             cag_copy(off).wait_recv()
         pair_copy(1).start()
 
-    part_ref[0] = dot(lead(), lead(), TN)
+    gram_blocks(0, lead_ref[0], lead_ref[1], TN)
     scatter_start(0)
     c_part[...] = dot(lead(), panels_ref[...], TN)
     pair_copy(0).start()
@@ -276,7 +282,7 @@
     cross_scatter()
     chol_inverse(gram_ref.at[0], inv_ref.at[0], cross_gather)
     basis = dot(inv_ref[0], lead(), NT)
-    part_ref[1] = dot(basis, basis, NT)
+    gram_blocks(1, basis[:PANEL], basis[PANEL:], NT)
     scatter_start(1)
     cross_pair()
     scatter_finish(1)
@@ -326,9 +332,9 @@
         out_specs=pl.BlockSpec(memory_space=vmem),
         scratch_shapes=[
             vmem((2, rows, PANEL), f32),
-            vmem((2, LEAD, LEAD), f32),
-            vmem((2, N_ROW - 1, N_ROW, LEAD), f32),
-            vmem((2, LEAD, LEAD), f32),
+            vmem((2, GRAM, PANEL), f32),
+            vmem((2, N_ROW - 1, GRAM // N_ROW, PANEL), f32),
+            vmem((2, GRAM, PANEL), f32),
             vmem((2, LEAD, LEAD), f32),
             vmem((LEAD, width), f32),
             vmem((PANEL, width), f32),

time: 110 us -> 106 us (0.964)
  Pallas kernels: 108 us -> 104 us
    pallas_call x1, Pallas kernels: 108 us -> 104 us  [local(): pl.pallas_call(kernel, out_shape=jax.ShapeDtypeStruct((LEAD, width), f32)...]
where the time goes in v5:
time: 106 us
  Pallas kernels  104 us (98%)
  local copies, waits for them, and re-layouts  1.87 us (2%)
    pallas_call x1, Pallas kernels, local(): pl.pallas_call(kernel, out_shape=jax.ShapeDtypeStruct((LEAD, width), f32)...  104 us

profile of v5, /device:TPU:45, one launch (start us, length us, event | category | flops | bytes accessed | tf_op | source)
XLA Modules:
  0.0 105.9 jit_solution(3955873224848928338)
XLA Ops:
  0.0 104.0 %shard_map.17 = f32[256,512]{1,0:T(8,128)} custom-call(f32[512,512]{1,0:T(8,128)} %panels_ref.1), custom_call_target="tpu_custom_call" | custom-call | tf_op jit(solution)/shard_map/pallas_call | solution.py:328
  104.0 1.9 %copy.3 = f32[256,512]{1,0:T(8,128)} copy(f32[256,512]{1,0:T(8,128)} %shard_map.17) | data formatting | bytes 1048576

commit v6 on v5

--- a/solution.py
+++ b/solution.py
@@ -111,7 +111,7 @@
         return {"row": lax.rem(me + off, N_ROW)}
 
     partner = {"row": z * 2 + 1 - core}
-    near = [at_xy(0, 1), at_xy(0, -1), at_xy(1, 0), at_xy(-1, 0)]
+    near = [at_xy(0, 1), at_xy(0, -1), at_xy(1, 0), at_xy(-1, 0), at_xy(2, 0)]
 
     barrier = pltpu.get_barrier_semaphore()
     for off in far_first(N_ROW):
@@ -127,12 +127,12 @@
         d = lax.rem(y - panel + Y_SIZE, Y_SIZE)
         up, down = d <= 3, (d == 0) | (d >= 6)
         if tree == 0:
-            return [(x == 0) & up, (x == 0) & down, x <= 1, x == 0]
-        return [(x != 0) & up, (x != 0) & down, (d == 0) & (x <= 1),
-                ((d == 0) & (x == 0)) | ((d != 0) & (x == 1))]
+            return [(x == 0) & up, (x == 0) & down, x == 0, x == 0, x == 0]
+        return [(x != 0) & up, (x != 0) & down, (d == 0) & (x == 0),
+                ((d == 0) & (x == 0)) | ((d != 0) & (x == 1)), (d == 0) & (x == 0)]
 
     def relays(cond):
-        return cond[0] | cond[1] | cond[2] | cond[3]
+        return cond[0] | cond[1] | cond[2] | cond[3] | cond[4]
 
     def hop(k, tree, panel, way, own):
         rows = pl.ds(pl.multiple_of(tree * half_rows + k * size, size), size)
@@ -149,7 +149,7 @@
             def _():
                 for tree in range(2):
                     cond = sends(tree, panel)
-                    for way in range(4):
+                    for way in range(5):
                         @pl.when(cond[way])
                         def _():
                             hop(k, tree, panel, way, True).start()
@@ -163,7 +163,7 @@
                 @pl.when((col != panel) & relays(cond))
                 def _():
                     hop(k, tree, panel, 0, False).wait_recv()
-                    for way in range(4):
+                    for way in range(5):
                         @pl.when(cond[way])
                         def _():
                             hop(k, tree, panel, way, False).start()
@@ -312,7 +312,7 @@
         for tree in range(2):
             for panel in range(2):
                 cond = sends(tree, panel)
-                for way in range(4):
+                for way in range(5):
                     @pl.when(cond[way])
                     def _():
                         hop(k, tree, panel, way, False).wait_send()
@@ -341,7 +341,7 @@
             vmem((PANEL, width), f32),
             vmem((N_Z - 1, LEAD // 2 // N_Z, width), f32),
             vmem((LEAD, width), f32),
-            dma((CHUNKS * 4, 4)), dma((CHUNKS * 4,)),
+            dma((CHUNKS * 4, 5)), dma((CHUNKS * 4,)),
             dma((2, N_ROW - 1)), dma((2, N_ROW - 1)),
             dma((2, N_ROW - 1)), dma((2, N_ROW - 1)),
             dma((2,)), dma((2,)),

time: 106 us -> 104 us (0.981)
  the two profiles are of different devices: /device:TPU:45 before, /device:TPU:41 now
where the time goes in v6:
time: 104 us
  Pallas kernels  102 us (98%)
  local copies, waits for them, and re-layouts  1.87 us (2%)
    pallas_call x1, Pallas kernels, local(): pl.pallas_call(kernel, out_shape=jax.ShapeDtypeStruct((LEAD, width), f32)...  102 us

profile of v6, /device:TPU:41, one launch (start us, length us, event | category | flops | bytes accessed | tf_op | source)
XLA Modules:
  0.0 104.0 jit_solution(16590193788972472902)
XLA Ops:
  0.0 102.1 %shard_map.17 = f32[256,512]{1,0:T(8,128)} custom-call(f32[512,512]{1,0:T(8,128)} %panels_ref.1), custom_call_target="tpu_custom_call" | custom-call | tf_op jit(solution)/shard_map/pallas_call | solution.py:328
  102.1 1.9 %copy.3 = f32[256,512]{1,0:T(8,128)} copy(f32[256,512]{1,0:T(8,128)} %shard_map.17) | data formatting | bytes 1048576
